TPU v7x, 512 devices: a whole 4x8x8 slice. The times are simulated.
512 devices in a mesh: dp: 64 (over z, y_hi, core), stat: 8 (over x, y_lo).
Axes of the slice: x: 4, y: 8 (y_hi: 4, y_lo: 2; y = y_hi * 2 + y_lo), z: 8, core: 2. Of those that a mesh axis runs over, the one named last changes fastest.
Arguments:
- activations: bfloat16 [65536, 8192], P('dp'), may hold values from -16 to 16
- out_grads: bfloat16 [65536, 1024], P('dp', 'stat'), may hold values from -0.0234375 to 0.0234375
- stat_old: float32 [192, 128, 128], P('dp'), may hold values from -0.24 to 0.24
- pattern: int32 [192, 2], replicated, may hold values from 0 to 63, as said below
- holders: int32 [192], replicated, may hold values from 0 to 63, as said below
Outputs:
- direction: float32 [8192, 1024], P('dp', 'stat')
- statistics: float32 [192, 128, 128], P('dp', 'stat')
Inputs may be any that keep to these rules, and one draw needn't show every extreme that they name: `pattern`: every diagonal pair (a, a) for a in 0 to 63 appears exactly once; every other entry has different row and column blocks; half of those are band pairs (column block next to the row block, cyclically), the rest reach anywhere. `holders`: every dp index holds exactly 3 entries; the diagonal entry (a, a) is held by the dp index whose weight rows contain row a * 128.
All inputs are finite; a program needn't handle non-finite values.
Results may differ from a plain program's by a relative error of at most 0.003.
Values may be sent and summed in bfloat16 or wider, within the bound.
No kernel may reach another device: no remote copies, remote signals or barrier semaphores. Data moves between devices by JAX's collectives and lax.ppermute only.
A program may use at most 192 MiB of HBM per device.

v0:
```python
import jax
import jax.numpy as jnp
from jax import lax
from jax.sharding import PartitionSpec as P

ITERS = 5
beta_stat = 0.6
damping = 0.75


def inverse_root(matrix):
    size = matrix.shape[0]
    eye = jnp.eye(size, dtype=matrix.dtype)
    sym = 0.5 * (matrix + matrix.T) + damping * eye
    scale = jnp.sqrt(jnp.sum(sym * sym))
    current = sym / scale
    result = eye
    for sweep in range(ITERS):
        factor = (5.0 * eye - current) * 0.25
        result = jnp.dot(result, factor, precision=lax.Precision.HIGHEST)
        square = jnp.dot(factor, factor, precision=lax.Precision.HIGHEST)
        fourth = jnp.dot(square, square, precision=lax.Precision.HIGHEST)
        current = jnp.dot(fourth, current, precision=lax.Precision.HIGHEST)
    return result * scale ** (-0.25)


def per_device(activations, out_grads, stat_old, pattern, holders):
    position = lax.axis_index("dp")
    stat_pos = lax.axis_index("stat")
    stat_count = lax.axis_size("stat")
    group_count = lax.axis_size("dp")
    block = stat_old.shape[2]
    held = stat_old.shape[0]
    width_cols = out_grads.shape[1]
    total_cols = width_cols * stat_count
    own_rows = activations.shape[1] // group_count
    own_panels = own_rows // block
    share_rows = block // stat_count
    partial_value = lax.dot_general(
        activations, out_grads, (((0,), (0,)), ((), ())), preferred_element_type=jnp.float32
    )
    grad_own = lax.psum_scatter(partial_value, "dp", scatter_dimension=0, tiled=True)
    grad_b = grad_own.astype(jnp.bfloat16)
    grad_full = lax.all_gather(grad_b, "dp", axis=0, tiled=True)
    entries = jnp.arange(holders.shape[0], dtype=jnp.int32)
    same_holder = holders[None, :] == holders[:, None]
    earlier = entries[None, :] < entries[:, None]
    within = jnp.sum((same_holder & earlier).astype(jnp.int32), axis=1)
    slot_ids = jnp.arange(held, dtype=jnp.int32)
    picked = ((holders[None, :] == position) & (within[None, :] == slot_ids[:, None])).astype(
        jnp.int32
    )
    row_blocks = jnp.sum(picked * pattern[None, :, 0], axis=1)
    col_blocks = jnp.sum(picked * pattern[None, :, 1], axis=1)

    def panel_at(index):
        return lax.dynamic_slice_in_dim(grad_full, index * block, block, 0)

    first = jax.vmap(panel_at)(row_blocks)
    second = jax.vmap(panel_at)(col_blocks)
    partial_gram = jnp.einsum("jrc,jsc->jrs", first, second, preferred_element_type=jnp.float32)
    panel_ids = position * own_panels + jnp.arange(own_panels, dtype=jnp.int32)
    select = (
        (row_blocks[None, :] == panel_ids[:, None]) & (col_blocks[None, :] == panel_ids[:, None])
    ).astype(jnp.float32)
    gram = lax.psum(partial_gram, "stat") / total_cols
    new_full = beta_stat * stat_old + (1.0 - beta_stat) * gram
    statistics = lax.dynamic_slice_in_dim(new_full, stat_pos * share_rows, share_rows, 1)
    diag_full = jnp.einsum("ij,jrs->irs", select, new_full, precision=lax.Precision.HIGHEST)
    roots = jax.vmap(inverse_root)(diag_full)
    stacked = grad_b.reshape(own_panels, block, width_cols).astype(jnp.float32)
    direction = jnp.einsum("irs,isc->irc", roots, stacked, precision=lax.Precision.HIGHEST).reshape(
        own_rows, width_cols
    )
    return (direction, statistics)


def solution(mesh):
    placed = (P("dp", None), P("dp", "stat"), P("dp", None, None), P(), P())
    return jax.shard_map(
        per_device,
        mesh=mesh,
        in_specs=placed,
        out_specs=(P("dp", "stat"), P("dp", "stat", None)),
        check_vma=False,
    )
```

profile of v0, /device:TPU:16, one launch (start us, length us, event | category | flops | bytes accessed | tf_op | source)
XLA Modules:
  0.0 372.1 jit_solution(4225835935777401481)
XLA Ops:
  7.2 0.0 copy-start
  7.2 0.0 reduce-scatter.2.cloned.1.call-start
  7.2 0.9 copy-done
  8.1 10.1 %fusion.82 = f32[8192,128]{1,0:T(8,128)} fusion(bf16[1024,8192]{1,0:T(8,128)(2,1)} %param.5, bf16[1024,128]{1,0:T(8,128)(2,1)S(1)} %copy-done), kind=kOutput, calls=%fused_computation.101 | convolution fusion | flops 2147483648 | bytes 21233664 | tf_op jit(solution)/shard_map/dot_general | solution.py:39
  18.2 0.0 copy-start.3
  18.2 0.0 reduce-scatter.2.cloned.1.call-update
  18.2 0.0 all-gather.2.cloned.1.call-start
  18.3 161.4 %reduce-scatter.2.cloned.1.call-done = f32[128,128]{1,0:T(8,128)} async-done(((f32[8192,128]{1,0:T(8,128)}), f32[128,128]{1,0:T(8,128)}) %reduce-scatter.2.cloned.1.call-update) | async-done | bytes 65552 | tf_op jit(solution)/shard_map/reduce_scatter | solution.py:42
  179.7 1.5 convert_element_type.5
  181.2 0.0 all-gather.2.cloned.1.call-update
  181.2 0.0 all-reduce.4.cloned.1.call-start
  181.3 0.0 copy-done.3
  181.3 0.2 convert_reduce_fusion
  181.5 0.0 copy-done.4
  181.5 0.1 select_reduce_fusion
  181.7 82.5 %all-gather.2.cloned.1.call-done = bf16[8192,128]{1,0:T(8,128)(2,1)} async-done(((bf16[128,128]{1,0:T(8,128)(2,1)}), bf16[8192,128]{1,0:T(8,128)(2,1)}) %all-gather.2.cloned.1.call-update) | async-done | bytes 2097168 | tf_op jit(solution)/shard_map/all_gather | solution.py:44
  264.2 5.7 %while.2 = (s32[]{:T(128)}, bf16[8192,128]{1,0:T(8,128)(2,1)}, s32[3,2]{0,1:T(2,128)S(1)}, bf16[3,128,128]{2,1,0:T(8,128)(2,1)S(1)}, s32[]{:T(128)}) while((s32[]{:T(128)}, bf16[8192,128]{1,0:T(8,128)(2,1)}, s32[3,2]{0,1:T(2,128)S(1)}, bf16[3,128,128]{2,1,0:T(8,128)(2,1)S(1)}, s32[]{:T(128)}) %tuple.34), condition=%wide.while_cond, body=%wide.while_body.sunk | while | flops 2 | bytes 65641 | solution.py:57
  264.3 0.1 constant_dynamic-slice_fusion.5
  264.3 0.5 slice.34
  264.8 1.3 bitcast_dynamic-update-slice_fusion.4
  266.2 0.1 constant_dynamic-slice_fusion.5
  266.2 0.5 slice.34
  266.7 1.3 bitcast_dynamic-update-slice_fusion.4
  268.1 0.1 constant_dynamic-slice_fusion.5
  268.2 0.5 slice.34
  268.6 1.3 bitcast_dynamic-update-slice_fusion.4
  270.0 6.1 %while.3 = (s32[]{:T(128)}, bf16[8192,128]{1,0:T(8,128)(2,1)}, s32[3,2]{0,1:T(2,128)S(1)}, bf16[3,128,128]{2,1,0:T(8,128)(2,1)S(1)}, s32[]{:T(128)}) while((s32[]{:T(128)}, bf16[8192,128]{1,0:T(8,128)(2,1)}, s32[3,2]{0,1:T(2,128)S(1)}, bf16[3,128,128]{2,1,0:T(8,128)(2,1)S(1)}, s32[]{:T(128)}) %tuple.46), condition=%wide.while_cond.1, body=%wide.while_body.1.sunk | while | flops 2 | bytes 65641 | solution.py:57
  270.0 0.1 constant_dynamic-slice_fusion.6
  270.1 0.5 slice.35
  270.6 1.4 bitcast_dynamic-update-slice_fusion.5
  272.1 0.1 constant_dynamic-slice_fusion.6
  272.1 0.5 slice.35
  272.6 1.4 bitcast_dynamic-update-slice_fusion.5
  274.1 0.1 constant_dynamic-slice_fusion.6
  274.2 0.5 slice.35
  274.7 1.4 bitcast_dynamic-update-slice_fusion.5
  276.1 0.9 fusion.83
  277.0 0.0 all-reduce.4.cloned.1.call-update
  277.0 80.5 %all-reduce.4.cloned.1.call-done = f32[3,128,128]{2,1,0:T(8,128)} async-done(((f32[3,128,128]{2,1,0:T(8,128)}), f32[3,128,128]{2,1,0:T(8,128)}) %all-reduce.4.cloned.1.call-update) | async-done | bytes 196624 | tf_op jit(solution)/shard_map/psum | solution.py:66
  357.6 0.0 copy-done.2
  357.6 1.0 multiply_add_fusion
  358.5 0.5 fusion.1
  359.0 0.1 copy.10
  359.1 0.6 multiply_reduce_fusion
  360.4 0.2 fusion.11
  360.6 0.2 fusion.9
  360.8 0.2 fusion.84
  361.1 0.2 fusion.7
  361.3 0.2 fusion.23
  361.5 0.2 fusion.25
  361.7 0.2 fusion.85
  361.9 0.2 fusion.86
  362.1 0.2 fusion.19
  362.3 0.2 fusion.21
  362.6 0.2 fusion.87
  362.8 0.2 fusion.88
  363.0 0.2 fusion.15
  363.2 0.2 fusion.17
  363.4 0.2 fusion.89
  363.6 0.2 fusion
  363.9 0.2 convolution_multiply_fusion
  364.1 0.0 copy-done.1
  364.1 0.8 fusion.90
  364.9 0.6 constant_dynamic-slice_fusion.2
  (11 shorter events, 0.1 us)
Async XLA Ops:
  7.2 1.0 copy-start
  7.2 172.6 %reduce-scatter.2.cloned.1.call-start = ((), (), s32[]{:S(2)}) async-start(), calls=%async_computation.1 | async-start | bytes 4259840 | tf_op jit(solution)/shard_map/reduce_scatter | solution.py:42
  18.2 163.1 %copy-start.3 = (s32[192]{0:T(256)S(1)}, s32[192]{0:T(256)}, u32[]{:S(2)}) copy-start(s32[192]{0:T(256)} %param.9) | copy-start | bytes 2308
  18.2 163.3 %copy-start.4 = (s32[192,2]{0,1:T(2,128)S(1)}, s32[192,2]{0,1:T(2,128)}, u32[]{:S(2)}) copy-start(s32[192,2]{0,1:T(2,128)} %param.8) | copy-start | bytes 4612
  18.2 339.4 %copy-start.2 = (f32[3,128,128]{2,1,0:T(8,128)S(1)}, f32[3,128,128]{2,1,0:T(8,128)}, u32[]{:S(2)}) copy-start(f32[3,128,128]{2,1,0:T(8,128)} %param.7) | copy-start | bytes 589828
  18.2 246.0 %all-gather.2.cloned.1.call-start = ((), (), s32[]{:S(2)}) async-start(), calls=%async_computation.2 | async-start | bytes 2129920 | tf_op jit(solution)/shard_map/all_gather | solution.py:44
  181.2 182.9 %copy-start.1 = (bf16[128,128]{1,0:T(8,128)(2,1)S(1)}, bf16[128,128]{1,0:T(8,128)(2,1)}, u32[]{:S(2)}) copy-start(bf16[128,128]{1,0:T(8,128)(2,1)} %convert_element_type.5) | copy-start | bytes 98308
  181.2 176.3 %all-reduce.4.cloned.1.call-start = ((), (), s32[]{:S(2)}) async-start(), calls=%async_computation.3 | async-start | bytes 393216 | tf_op jit(solution)/shard_map/psum | solution.py:66
Sparse Core Ops, SparseCore 0:
  18.4 161.3 reduce-scatter.1
  183.7 80.5 all-gather.1
  277.1 80.3 all-reduce.3
where the time goes:
time: 373 us; the launch traced here: 372 us
  waiting for transfers between devices  325 us (87%)
  matrix products  15.7 us (4%)
  between operations  14.8 us (4%)
  local copies, waits for them, and re-layouts  13.4 us (4%)
    reduce_scatter x1, waiting for transfers between devices, per_device(): lax.psum_scatter(partial_value, 'dp', scatter_dimension=0, tiled=True)  161 us
    all_gather x1, waiting for transfers between devices, per_device(): grad_full = lax.all_gather(grad_b, 'dp', axis=0, tiled=True)  82.5 us
    psum x1, waiting for transfers between devices, per_device(): gram = lax.psum(partial_gram, 'stat') / total_cols  80.5 us
    gather x18, local copies, waits for them, and re-layouts  11.7 us
    dot_general x1, matrix products, per_device(): lax.dot_general(activations, out_grads, (((0,), (0,)), ((), ())), preferr...  10.1 us
  transfers between devices with their start and end apart: 3, of which 3 were waited for; matrix products, arithmetic and copies ran while one was open for 0% of the time, Pallas kernels for 0%

commit v1 on v0

--- a/solution.py
+++ b/solution.py
@@ -63,7 +63,7 @@
     select = (
         (row_blocks[None, :] == panel_ids[:, None]) & (col_blocks[None, :] == panel_ids[:, None])
     ).astype(jnp.float32)
-    gram = lax.psum(partial_gram, "stat") / total_cols
+    gram = jnp.sum(lax.all_gather(partial_gram, "stat"), axis=0) / total_cols
     new_full = beta_stat * stat_old + (1.0 - beta_stat) * gram
     statistics = lax.dynamic_slice_in_dim(new_full, stat_pos * share_rows, share_rows, 1)
     diag_full = jnp.einsum("ij,jrs->irs", select, new_full, precision=lax.Precision.HIGHEST)

time: 373 us -> 337 us (0.903)
  the two profiles are of different devices: /device:TPU:16 before, /device:TPU:1 now
where the time goes in v1:
time: 337 us
  waiting for transfers between devices  288 us (85%)
  matrix products  15.7 us (5%)
  between operations  14.8 us (4%)
  local copies, waits for them, and re-layouts  13.4 us (4%)
  other arithmetic  3.99 us (1%)
    reduce_scatter x1, waiting for transfers between devices, per_device(): lax.psum_scatter(partial_value, 'dp', scatter_dimension=0, tiled=True)  158 us
    all_gather x1, waiting for transfers between devices, per_device(): grad_full = lax.all_gather(grad_b, 'dp', axis=0, tiled=True)  88 us
    all_gather x1, waiting for transfers between devices, per_device(): gram = jnp.sum(lax.all_gather(partial_gram, 'stat'), axis=0) / total_cols  42.5 us
    gather x18, local copies, waits for them, and re-layouts  11.7 us
    dot_general x1, matrix products, per_device(): lax.dot_general(activations, out_grads, (((0,), (0,)), ((), ())), preferr...  10.1 us
  transfers between devices with their start and end apart: 3, of which 3 were waited for; matrix products, arithmetic and copies ran while one was open for 0% of the time, Pallas kernels for 0%

profile of v1, /device:TPU:1, one launch (start us, length us, event | category | flops | bytes accessed | tf_op | source)
XLA Modules:
  0.0 336.5 jit_solution(13254435467371964618)
XLA Ops:
  7.2 0.0 copy-start
  7.2 0.0 reduce-scatter.2.cloned.1.call-start
  7.2 0.9 copy-done
  8.1 10.1 %fusion.82 = f32[8192,128]{1,0:T(8,128)} fusion(bf16[1024,8192]{1,0:T(8,128)(2,1)} %param.5, bf16[1024,128]{1,0:T(8,128)(2,1)S(1)} %copy-done), kind=kOutput, calls=%fused_computation.101 | convolution fusion | flops 2147483648 | bytes 21233664 | tf_op jit(solution)/shard_map/dot_general | solution.py:39
  18.2 0.0 copy-start.3
  18.2 0.0 reduce-scatter.2.cloned.1.call-update
  18.2 0.0 all-gather.4.cloned.1.call-start
  18.3 157.9 %reduce-scatter.2.cloned.1.call-done = f32[128,128]{1,0:T(8,128)} async-done(((f32[8192,128]{1,0:T(8,128)}), f32[128,128]{1,0:T(8,128)}) %reduce-scatter.2.cloned.1.call-update) | async-done | bytes 65552 | tf_op jit(solution)/shard_map/reduce_scatter | solution.py:42
  176.2 1.5 convert_element_type.5
  177.6 0.0 all-gather.4.cloned.1.call-update
  177.7 0.0 all-gather.6.cloned.1.call-start
  177.7 0.0 copy-done.3
  177.7 0.2 convert_reduce_fusion
  177.9 0.0 copy-done.4
  177.9 0.1 select_reduce_fusion
  178.1 88.0 %all-gather.4.cloned.1.call-done = bf16[8192,128]{1,0:T(8,128)(2,1)} async-done(((bf16[128,128]{1,0:T(8,128)(2,1)}), bf16[8192,128]{1,0:T(8,128)(2,1)}) %all-gather.4.cloned.1.call-update) | async-done | bytes 2097168 | tf_op jit(solution)/shard_map/all_gather | solution.py:44
  266.1 5.7 %while.2 = (s32[]{:T(128)}, bf16[8192,128]{1,0:T(8,128)(2,1)}, s32[3,2]{0,1:T(2,128)S(1)}, bf16[3,128,128]{2,1,0:T(8,128)(2,1)S(1)}, s32[]{:T(128)}) while((s32[]{:T(128)}, bf16[8192,128]{1,0:T(8,128)(2,1)}, s32[3,2]{0,1:T(2,128)S(1)}, bf16[3,128,128]{2,1,0:T(8,128)(2,1)S(1)}, s32[]{:T(128)}) %tuple.34), condition=%wide.while_cond, body=%wide.while_body.sunk | while | flops 2 | bytes 65641 | solution.py:57
  266.1 0.1 constant_dynamic-slice_fusion.5
  266.2 0.5 slice.34
  266.7 1.3 bitcast_dynamic-update-slice_fusion.4
  268.1 0.1 constant_dynamic-slice_fusion.5
  268.1 0.5 slice.34
  268.6 1.3 bitcast_dynamic-update-slice_fusion.4
  270.0 0.1 constant_dynamic-slice_fusion.5
  270.0 0.5 slice.34
  270.5 1.3 bitcast_dynamic-update-slice_fusion.4
  271.9 6.1 %while.3 = (s32[]{:T(128)}, bf16[8192,128]{1,0:T(8,128)(2,1)}, s32[3,2]{0,1:T(2,128)S(1)}, bf16[3,128,128]{2,1,0:T(8,128)(2,1)S(1)}, s32[]{:T(128)}) while((s32[]{:T(128)}, bf16[8192,128]{1,0:T(8,128)(2,1)}, s32[3,2]{0,1:T(2,128)S(1)}, bf16[3,128,128]{2,1,0:T(8,128)(2,1)S(1)}, s32[]{:T(128)}) %tuple.46), condition=%wide.while_cond.1, body=%wide.while_body.1.sunk | while | flops 2 | bytes 65641 | solution.py:57
  271.9 0.1 constant_dynamic-slice_fusion.6
  272.0 0.5 slice.35
  272.5 1.4 bitcast_dynamic-update-slice_fusion.5
  273.9 0.1 constant_dynamic-slice_fusion.6
  274.0 0.5 slice.35
  274.5 1.4 bitcast_dynamic-update-slice_fusion.5
  276.0 0.1 constant_dynamic-slice_fusion.6
  276.1 0.5 slice.35
  276.6 1.4 bitcast_dynamic-update-slice_fusion.5
  278.0 0.9 fusion.83
  278.9 0.0 all-gather.6.cloned.1.call-update
  278.9 42.5 %all-gather.6.cloned.1.call-done = f32[24,128,128]{2,1,0:T(8,128)} async-done(((f32[3,128,128]{2,1,0:T(8,128)}), f32[24,128,128]{2,1,0:T(8,128)}) %all-gather.6.cloned.1.call-update) | async-done | bytes 1572880 | tf_op jit(solution)/shard_map/all_gather | solution.py:66
  321.4 1.5 reduce_sum.48
  322.9 0.0 copy-done.2
  323.0 0.5 fusion.1
  323.5 0.1 copy.11
  323.5 0.6 multiply_reduce_fusion
  324.9 0.2 fusion.11
  325.1 0.2 fusion.9
  325.3 0.2 fusion.84
  325.5 0.2 fusion.7
  325.7 0.2 fusion.23
  325.9 0.2 fusion.25
  326.2 0.2 fusion.85
  326.4 0.2 fusion.86
  326.6 0.2 fusion.19
  326.8 0.2 fusion.21
  327.0 0.2 fusion.87
  327.2 0.2 fusion.88
  327.4 0.2 fusion.15
  327.6 0.2 fusion.17
  327.9 0.2 fusion.89
  328.1 0.2 fusion
  328.3 0.2 convolution_multiply_fusion
  328.6 0.0 copy-done.1
  328.6 0.8 fusion.90
  329.4 0.6 constant_dynamic-slice_fusion.2
  (12 shorter events, 0.1 us)
Async XLA Ops:
  7.2 1.0 copy-start
  7.2 169.0 %reduce-scatter.2.cloned.1.call-start = ((), (), s32[]{:S(2)}) async-start(), calls=%async_computation.1 | async-start | bytes 4259840 | tf_op jit(solution)/shard_map/reduce_scatter | solution.py:42
  18.2 159.5 %copy-start.3 = (s32[192]{0:T(256)S(1)}, s32[192]{0:T(256)}, u32[]{:S(2)}) copy-start(s32[192]{0:T(256)} %param.9) | copy-start | bytes 2308
  18.2 159.7 %copy-start.4 = (s32[192,2]{0,1:T(2,128)S(1)}, s32[192,2]{0,1:T(2,128)}, u32[]{:S(2)}) copy-start(s32[192,2]{0,1:T(2,128)} %param.8) | copy-start | bytes 4612
  18.2 304.7 %copy-start.2 = (f32[3,128,128]{2,1,0:T(8,128)S(1)}, f32[3,128,128]{2,1,0:T(8,128)}, u32[]{:S(2)}) copy-start(f32[3,128,128]{2,1,0:T(8,128)} %param.7) | copy-start | bytes 589828
  18.2 247.9 %all-gather.4.cloned.1.call-start = ((), (), s32[]{:S(2)}) async-start(), calls=%async_computation.2 | async-start | bytes 2129920 | tf_op jit(solution)/shard_map/all_gather | solution.py:44
  177.6 150.9 %copy-start.1 = (bf16[128,128]{1,0:T(8,128)(2,1)S(1)}, bf16[128,128]{1,0:T(8,128)(2,1)}, u32[]{:S(2)}) copy-start(bf16[128,128]{1,0:T(8,128)(2,1)} %convert_element_type.5) | copy-start | bytes 98308
  177.7 143.8 %all-gather.6.cloned.1.call-start = ((), (), s32[]{:S(2)}) async-start(), calls=%async_computation.3 | async-start | bytes 1769472 | tf_op jit(solution)/shard_map/all_gather | solution.py:66
Sparse Core Ops, SparseCore 0:
  18.4 157.7 reduce-scatter.1
  180.1 85.9 all-gather.3
  279.0 42.3 all-gather.5
